TPU v7x, 32 devices: a whole 2x2x4 slice. The times are simulated.
32 devices in a mesh: pipe: 4 (over y, core), section: 4 (over z), tensor: 2 (over x).
Axes of the slice: x: 2, y: 2, z: 4, core: 2. Of those that a mesh axis runs over, the one named last changes fastest.
Arguments:
- bounds: int32 [2, 3], replicated, may hold values from 0 to 2, as said below
- saved_inputs: bfloat16 [4, 4, 2, 256, 1024], P('pipe', 'section', None, 'tensor')
- w_in: bfloat16 [4, 4, 2, 1024, 1024], P('pipe', 'section'), as said below
- w_out: bfloat16 [4, 4, 2, 1024, 1024], P('pipe', 'section')
- top_grad: bfloat16 [4, 2, 256, 1024], P('pipe', None, 'tensor'), may hold values from -0.125 to 0.125
Outputs:
- grad_in: float32 [4, 512, 1024], P('section', 'pipe', 'tensor')
- grad_out: float32 [4, 512, 1024], P('section', 'pipe', 'tensor')
Inputs may be any that keep to these rules, and one draw needn't show every extreme that they name: Row p of bounds starts at 0 and never falls; each relay either uses all 2 sections with one layer each, or gives one or two layers to each of its first 1 section with its later entries equal to 2; at least one relay is of each kind. `w_in`: for k < bounds[p, s+1] - bounds[p, s], slot k of entries [2p + a, 2s + b] holds layer bounds[p, s] + k, the same for every a and b; a layer's weights are the same in every relay.
All inputs are finite; a program needn't handle non-finite values.
Results may differ from a plain program's by a relative error of at most 0.014.
Values may be sent and summed in bfloat16 or wider, within the bound.
No kernel may reach another device: no remote copies, remote signals or barrier semaphores. Data moves between devices by JAX's collectives and lax.ppermute only.
A program may use at most 64 MiB of HBM per device.

v0:
```python
import jax
import jax.numpy as jnp
from jax import lax
from jax.sharding import PartitionSpec as P

EPS = 1e-05


def shifted(value, axis, steps):
    count = lax.axis_size(axis)
    pairs = [(source, (source + steps) % count) for source in range(count)]
    return lax.ppermute(value, axis, pairs)


def for_sending(shard):

    def short(part):
        return part.astype(jnp.bfloat16) if part.dtype == jnp.float32 else part

    return jax.tree.map(short, shard)


def partner(block, axis, bit):
    count = lax.axis_size(axis)
    route = []
    for low in range(count):
        high = low | 1 << bit
        if high != low and high < count:
            route += [(low, high), (high, low)]
    return lax.ppermute(block, axis, route)


def normalize(saved_rows):
    floats = saved_rows.astype(jnp.float32)
    row_scale = jnp.sqrt(jnp.mean(floats * floats, axis=-1, keepdims=True) + EPS)
    return (floats / row_scale, row_scale)


def layer_back(grad_next, unit_rows, row_scale, proj_in, proj_out):
    err_low = jnp.dot(grad_next, proj_out.T, preferred_element_type=jnp.float32).astype(
        jnp.bfloat16
    )
    pulled = jnp.dot(err_low, proj_in.T, preferred_element_type=jnp.float32)
    inner_mean = jnp.mean(pulled * unit_rows, axis=-1, keepdims=True)
    grad_here = (
        grad_next.astype(jnp.float32) + (pulled - unit_rows * inner_mean) / row_scale
    ).astype(jnp.bfloat16)
    return (grad_here, err_low)


def route_items(members, shifter, offset, occupied, positions, here_section, levels, sections):
    for bit_level in reversed(range(levels)):
        stride = 2**bit_level
        passed = offset // (2 * stride) * (2 * stride)
        present = occupied & ((positions[:, None] + passed) % sections == here_section)
        rising = offset // stride % 2 == 1
        send_mask = jnp.any(present & rising, axis=0)
        keep_mask = jnp.any(present & jnp.logical_not(rising), axis=0)
        outgoing = tuple(
            (
                jnp.where(send_mask[:, None, None], member, jnp.zeros_like(member))
                for member in members
            )
        )
        arrived = shifter(outgoing, stride)
        members = tuple(
            (
                jnp.where(keep_mask[:, None, None], member, jnp.zeros_like(member)) + landed
                for member, landed in zip(members, arrived)
            )
        )
    return members


def body(bounds, saved_inputs, w_in, w_out, top_grad):
    sections = lax.axis_size("section") // 2
    tensors = lax.axis_size("tensor")
    pipe_index = lax.axis_index("pipe")
    section_index = lax.axis_index("section")
    tensor_index = lax.axis_index("tensor")
    position = section_index // 2
    token_half = section_index % 2
    boundary = lax.dynamic_index_in_dim(bounds, pipe_index // 2, 0, keepdims=False)
    counts = boundary[1:] - boundary[:-1]
    layers_here = lax.dynamic_index_in_dim(counts, position, 0, keepdims=False)
    saved_rows = saved_inputs[0, 0]
    proj_in = w_in[0, 0]
    proj_out = w_out[0, 0]
    slot_count = saved_rows.shape[0]
    row_count = saved_rows.shape[1]
    model_width = saved_rows.shape[2]
    inner_width = proj_in.shape[2]
    unit_rows, scales = normalize(saved_rows)
    unit_low = unit_rows.astype(jnp.bfloat16)
    value_low = jnp.einsum(
        "kre,kea->kra", unit_low, proj_in, preferred_element_type=jnp.float32
    ).astype(jnp.bfloat16)
    positions = jnp.arange(sections, dtype=jnp.int32)
    slot_ids = jnp.arange(slot_count, dtype=jnp.int32)
    occupied = slot_ids[None, :] < counts[:, None]
    layer_of = boundary[:-1, None] + slot_ids[None, :]
    offset = (layer_of + 1 - positions[:, None]) % sections
    levels = min((sections - 3 * sections // 4 + 1).bit_length(), (sections - 1).bit_length())
    top_rows = lax.dynamic_index_in_dim(top_grad[0], token_half, 0, keepdims=False)

    def run_section(incoming):

        def upper_layer(grad_top):
            return layer_back(grad_top, unit_rows[1], scales[1], proj_in[1], proj_out[1])

        def lower_layer(grad_top):
            return layer_back(grad_top, unit_rows[0], scales[0], proj_in[0], proj_out[0])

        def no_layer(grad_top):
            return (grad_top, jnp.zeros((row_count, inner_width), jnp.bfloat16))

        lower_start, upper_err = lax.cond(layers_here == 2, upper_layer, no_layer, incoming)
        result, lower_err = lax.cond(layers_here >= 1, lower_layer, no_layer, lower_start)
        return (result, jnp.stack([lower_start, incoming]), jnp.stack([lower_err, upper_err]))

    def loop_turn(turn_index, carried):
        incoming = shifted(carried[0], "section", -2)
        return lax.cond(
            position == sections - 1 - turn_index,
            lambda arriving, kept: run_section(arriving),
            lambda arriving, kept: kept,
            incoming,
            carried,
        )

    start_rows = jnp.where(position == 0, top_rows, jnp.zeros_like(top_rows))
    carried = (
        start_rows,
        jnp.zeros((slot_count, row_count, model_width), jnp.bfloat16),
        jnp.zeros((slot_count, row_count, inner_width), jnp.bfloat16),
    )
    carried = lax.fori_loop(0, sections, loop_turn, carried)
    grads_slots = carried[1]
    errors = carried[2]
    unit_got, value_got, err_got, grad_got = route_items(
        (unit_low, value_low, errors, grads_slots),
        lambda members, stride: jax.tree.map(
            lambda part, own: part.astype(own.dtype),
            shifted(for_sending(members), "section", 2 * stride),
            members,
        ),
        offset,
        occupied,
        positions,
        position,
        levels,
        sections,
    )
    owner_slot = jnp.sum(
        jnp.where(occupied & ((layer_of + 1) % sections == position), slot_ids[None, :], 0)
    )
    unit_own = lax.dynamic_index_in_dim(unit_got, owner_slot, 0, keepdims=False)
    value_own = lax.dynamic_index_in_dim(value_got, owner_slot, 0, keepdims=False)
    err_own = lax.dynamic_index_in_dim(err_got, owner_slot, 0, keepdims=False)
    grad_own = lax.dynamic_index_in_dim(grad_got, owner_slot, 0, keepdims=False)
    in_cols = inner_width // tensors
    out_cols = model_width // tensors
    unit_piece = lax.all_gather(unit_own, "tensor", axis=0, tiled=True)
    value_piece = lax.all_gather(value_own, "tensor", axis=0, tiled=True)
    err_piece = lax.all_gather(err_own, "tensor", axis=0, tiled=True)
    grad_piece = lax.all_gather(grad_own, "tensor", axis=0, tiled=True)
    err_cols = lax.dynamic_slice_in_dim(err_piece, tensor_index * in_cols, in_cols, 1)
    grad_cols = lax.dynamic_slice_in_dim(grad_piece, tensor_index * out_cols, out_cols, 1)
    totals = (
        jnp.dot(unit_piece.T, err_cols, preferred_element_type=jnp.float32),
        jnp.dot(value_piece.T, grad_cols, preferred_element_type=jnp.float32),
    )
    half_model = model_width // 2
    half_inner = inner_width // 2
    mine_in = lax.dynamic_slice_in_dim(totals[0], token_half * half_model, half_model, 0)
    other_in = lax.dynamic_slice_in_dim(totals[0], (1 - token_half) * half_model, half_model, 0)
    mine_out = lax.dynamic_slice_in_dim(totals[1], token_half * half_inner, half_inner, 0)
    other_out = lax.dynamic_slice_in_dim(totals[1], (1 - token_half) * half_inner, half_inner, 0)
    landed_in, landed_out = partner((other_in, other_out), "section", 0)
    grad_in_part, grad_out_part = (
        lax.psum_scatter(mine_in + landed_in, "pipe", scatter_dimension=0, tiled=True),
        lax.psum_scatter(mine_out + landed_out, "pipe", scatter_dimension=0, tiled=True),
    )
    return (grad_in_part[None], grad_out_part[None])


def solution(mesh):
    placed = (
        P(),
        P("pipe", "section", None, "tensor", None),
        P("pipe", "section", None, None, None),
        P("pipe", "section", None, None, None),
        P("pipe", None, "tensor", None),
    )
    return jax.shard_map(
        body,
        mesh=mesh,
        in_specs=placed,
        out_specs=(P("section", "pipe", "tensor"), P("section", "pipe", "tensor")),
        check_vma=False,
    )
```

profile of v0, /device:TPU:0, one launch (start us, length us, event | category | flops | bytes accessed | tf_op | source)
XLA Modules:
  0.0 233.2 jit_solution(8870678346075298713)
XLA Ops:
  7.2 0.0 copy-start
  7.2 0.0 copy-start.1
  7.2 0.0 copy-start.4
  7.2 0.0 reduce-scatter.3.cloned.1.call-start
  7.3 0.6 copy-done
  7.9 0.1 bitcast_subtract_fusion
  7.9 1.2 fusion.28
  9.2 0.1 and_reduce_fusion.1
  9.3 2.1 broadcast_select_fusion.3
  11.4 4.1 %collective-permute-start.1 = (bf16[2,128,1024]{2,1,0:T(8,128)(2,1)}, bf16[2,128,1024]{2,1,0:T(8,128)(2,1)}, u32[]{:S(2)}, u32[]{:S(2)}) collective-permute-start(bf16[2,128,1024]{2,1,0:T(8,128)(2,1)} %get-tuple-element.267), channel_id=1, source_target_pairs={{0,4},{2,6},{4,0},{6,2},{1,5},{3,7},{5,1},{7,3},{8,12},{10,14},{12... | collective-permute-start | bytes 1572872 | tf_op jit(solution)/shard_map/ppermute | solution.py:12
  15.5 0.0 copy-done.1
  15.5 0.1 convert_divide_fusion
  15.6 0.6 dynamic_slice.45
  16.2 0.0 copy-done.4
  16.2 0.7 select_bitcast_fusion
  17.0 0.1 broadcast.103
  17.0 0.1 broadcast.103.clone
  17.1 64.0 %while.17 = (s32[]{:T(128)}, bf16[128,1024]{1,0:T(8,128)(2,1)}, bf16[2,128,1024]{2,1,0:T(8,128)(2,1)S(1)}, bf16[2,128,1024]{2,1,0:T(8,128)(2,1)S(1)}, s32[]{:T(1...) while((s32[]{:T(128)}, bf16[128,1024]{1,0:T(8,128)(2,1)}, ...), condition=%wide.region_13.14_spmd, body=%wide.region_4.13_spmd.sunk | while | flops 1076625408 | bytes 18357676 | solution.py:137
  17.1 0.1 collective-permute-start
  17.2 32.9 %collective-permute-done = bf16[128,1024]{1,0:T(8,128)(2,1)S(1)} collective-permute-done((bf16[128,1024]{1,0:T(8,128)(2,1)}, bf16[128,1024]{1,0:T(8,128)(2,1)S(1)}, u32[]{:S(2)}, u32[]{:S(2)}) %collective-permute-start) | collective-permute-done | bytes 262176 | tf_op jit(solution)/shard_map/while/body/eval_jaxpr/ppermute | solution.py:12
  50.1 9.6 %collective-permute-start = (bf16[128,1024]{1,0:T(8,128)(2,1)}, bf16[128,1024]{1,0:T(8,128)(2,1)S(1)}, u32[]{:S(2)}, u32[]{:S(2)}) collective-permute-start(bf16[128,1024]{1,0:T(8,128)(2,1)} %get-tuple-element.372), channel_id=1, source_target_pairs={{0,4},{2,6},{4,0},{6,2},{1,5},{3,7},{5,1},{7,3},{8,12},{10,14},{12... | collective-permute-start | bytes 786440 | tf_op jit(solution)/shard_map/while/body/eval_jaxpr/ppermute | solution.py:12
  59.7 11.6 %collective-permute-done = bf16[128,1024]{1,0:T(8,128)(2,1)S(1)} collective-permute-done((bf16[128,1024]{1,0:T(8,128)(2,1)}, bf16[128,1024]{1,0:T(8,128)(2,1)S(1)}, u32[]{:S(2)}, u32[]{:S(2)}) %collective-permute-start) | collective-permute-done | bytes 262176 | tf_op jit(solution)/shard_map/while/body/eval_jaxpr/ppermute | solution.py:12
  71.2 9.8 %conditional.4 = ((bf16[128,1024]{1,0:T(8,128)(2,1)}, bf16[2,128,1024]{2,1,0:T(8,128)(2,1)S(1)}, bf16[2,128,1024]{2,1,0:T(8,128)(2,1)S(1)})) conditional(s32[]{:T(128)} %convert_element_type.62, (bf16[128,1024]{1,0:T(8,128)(2,1)}, bf16[2,128,1024]{2,1,0:T(8,128)(2,1)S(1)}, bf16[2,128,1024]{2,1,0:T(8,128)(2,1)S(1)}) %tuple.69, (s32[]{:T(128)}, ...), branch_computations={%region_5.5_spmd, %region_6.0_spmd} | conditional | flops 1076625408 | bytes 17308844 | solution.py:123
  72.5 0.8 conditional
  72.5 0.7 stack.18
  73.2 6.7 %conditional.1 = (bf16[128,1024]{1,0:T(8,128)(2,1)}, bf16[1,128,1024]{2,1,0:T(8,128)(2,1)}) conditional(s32[]{:T(128)} %convert_element_type.36, bf16[128,1024]{1,0:T(8,128)(2,1)S(1)} %get-tuple-element.221, (bf16[128,1024]{1,0:T(8,128)(2,1)S(1)}, bf16[2,1024,1024]{2,1,0:T(8,128)(2,1)}, bf16[2,1024,1024]{2,1,0:T(8,128)(2,1)}, ...), branch_computations={%region_10.9_spmd, %region_11.11_spmd} | conditional | flops 538050560 | bytes 7605776 | solution.py:118
  73.2 3.2 %fusion.20 = bf16[128,1024]{1,0:T(8,128)(2,1)} fusion(bf16[128,1024]{1,0:T(8,128)(2,1)S(1)} %get-tuple-element.210, bf16[2,1024,1024]{2,1,0:T(8,128)(2,1)} %get-tuple-element.211), kind=kOutput, calls=%fused_computation.22 | convolution fusion | flops 268566528 | bytes 2621440 | tf_op jit(solution)/shard_map/while/body/eval_jaxpr/cond/branch_1_fun/cond/branch_1_fun/dot_general | solution.py:40
  76.4 2.6 %fusion.23 = (f32[128]{0:T(128)S(1)}, f32[128,1024]{1,0:T(8,128)S(1)}) fusion(f32[2,128,1024]{2,1,0:T(8,128)S(1)} %get-tuple-element.213, bf16[128,1024]{1,0:T(8,128)(2,1)} %fusion.20, bf16[2,1024,1024]{2,1,0:T(8,128)(2,1)} %get-tuple-element.212), kind=kOutput, calls=%fused_computation.25 | convolution fusion | flops 268697472 | bytes 3408384 | tf_op jit(solution)/shard_map/while/body/eval_jaxpr/cond/branch_1_fun/cond/branch_1_fun/dot_general | solution.py:43
  79.0 0.9 fusion.27
  79.9 1.1 pad_maximum_fusion
  81.1 4.0 %broadcast_select_fusion = (bf16[2,128,1024]{2,1,0:T(8,128)(2,1)}, bf16[2,128,1024]{2,1,0:T(8,128)(2,1)S(1)}, bf16[2,128,1024]{2,1,0:T(8,128)(2,1)}, bf16[2,128,1024]{2,1,0:T(8,128)(2,1)}) fusion(bf16[2,128,1024]{2,1,0:T(8,128)(2,1)S(1)} %get-tuple-element.244, pred[2]{0:T(512)(128)(4,1)S(1)} %get-tuple-element.246, ...), kind=kOutput, calls=%fused_computation.44 | convolution fusion | flops 537919488 | bytes 7864322 | tf_op jit(solution)/shard_map/kre,kea->kra/dot_general | solution.py:95
  85.1 0.0 collective-permute-start.2
  85.1 0.7 fusion.42
  87.8 0.6 dynamic-slice.3
  88.4 0.0 collective-permute-done.1
  88.4 1.6 dynamic-slice_add_fusion.5
  90.0 8.5 %all-gather = bf16[1,256,1024]{2,1,0:T(8,128)(2,1)S(1)} all-gather(bf16[1,128,1024]{2,1,0:T(8,128)(2,1)S(1)} %dynamic-slice_add_fusion.5), channel_id=2, replica_groups=mesh['pipe'=4,'section'=4,'tensor'=2] {'tensor'}, dimensions={1}, use_global_device_ids=true | all-gather | bytes 786432 | tf_op jit(solution)/shard_map/all_gather | solution.py:163
  98.5 7.2 %collective-permute-done.2 = bf16[2,128,1024]{2,1,0:T(8,128)(2,1)S(1)} collective-permute-done((bf16[2,128,1024]{2,1,0:T(8,128)(2,1)S(1)}, bf16[2,128,1024]{2,1,0:T(8,128)(2,1)S(1)}, u32[]{:S(2)}, u32[]{:S(2)}) %collective-permute-start.2) | collective-permute-done | bytes 524320 | tf_op jit(solution)/shard_map/ppermute | solution.py:12
  105.7 0.7 dynamic-slice_add_fusion.4
  106.4 7.0 %all-gather.1 = bf16[1,256,1024]{2,1,0:T(8,128)(2,1)S(1)} all-gather(bf16[1,128,1024]{2,1,0:T(8,128)(2,1)S(1)} %dynamic-slice_add_fusion.4), channel_id=3, replica_groups=mesh['pipe'=4,'section'=4,'tensor'=2] {'tensor'}, dimensions={1}, use_global_device_ids=true | all-gather | bytes 786432 | tf_op jit(solution)/shard_map/all_gather | solution.py:165
  113.5 0.5 fusion.31
  113.9 1.1 constant_dynamic-slice_fusion.1
  115.0 0.0 collective-permute-start.3
  115.0 2.1 collective-permute-start.5
  117.2 0.0 copy-done.3
  117.2 0.8 collective-permute-start.4
  118.0 32.2 %collective-permute-done.5 = bf16[2,128,1024]{2,1,0:T(8,128)(2,1)} collective-permute-done((bf16[2,128,1024]{2,1,0:T(8,128)(2,1)}, bf16[2,128,1024]{2,1,0:T(8,128)(2,1)}, u32[]{:S(2)}, u32[]{:S(2)}) %collective-permute-start.5) | collective-permute-done | bytes 524320 | tf_op jit(solution)/shard_map/ppermute | solution.py:12
  150.2 1.6 dynamic-slice_add_fusion.2
  151.8 6.4 %collective-permute-done.3 = f32[512,512]{1,0:T(8,128)} collective-permute-done((f32[512,512]{1,0:T(8,128)}, f32[512,512]{1,0:T(8,128)}, u32[]{:S(2)}, u32[]{:S(2)}) %collective-permute-start.3) | collective-permute-done | bytes 1048608 | tf_op jit(solution)/shard_map/ppermute | solution.py:30
  158.3 2.4 %dynamic-slice_add_fusion.1 = f32[512,512]{1,0:T(8,128)} fusion(f32[512,512]{1,0:T(8,128)} %collective-permute-done.3, f32[1024,512]{1,0:T(8,128)S(1)} %fusion.31, s32[]{:T(128)S(6)} %select_n.129), kind=kLoop, calls=%fused_computation.39 | loop fusion | flops 262144 | bytes 3145732 | tf_op jit(solution)/shard_map/add | solution.py:181
  160.6 0.0 reduce-scatter.3.cloned.1.call-update
  160.7 0.0 reduce-scatter.5.cloned.1.call-start
  160.7 0.9 collective-permute-done.4
  161.6 1.6 dynamic-slice_add_fusion.3
  163.3 8.9 %all-gather.2 = bf16[1,256,1024]{2,1,0:T(8,128)(2,1)S(1)} all-gather(bf16[1,128,1024]{2,1,0:T(8,128)(2,1)S(1)} %dynamic-slice_add_fusion.3), channel_id=4, replica_groups=mesh['pipe'=4,'section'=4,'tensor'=2] {'tensor'}, dimensions={1}, use_global_device_ids=true | all-gather | bytes 786432 | tf_op jit(solution)/shard_map/all_gather | solution.py:164
  172.2 7.0 %all-gather.3 = bf16[1,256,1024]{2,1,0:T(8,128)(2,1)S(1)} all-gather(bf16[1,128,1024]{2,1,0:T(8,128)(2,1)S(1)} %dynamic-slice_add_fusion.2), channel_id=5, replica_groups=mesh['pipe'=4,'section'=4,'tensor'=2] {'tensor'}, dimensions={1}, use_global_device_ids=true | all-gather | bytes 786432 | tf_op jit(solution)/shard_map/all_gather | solution.py:166
  179.2 0.5 fusion.29
  179.7 0.1 constant_dynamic-slice_fusion
  179.8 0.1 collective-permute-start.6
  179.9 18.8 %collective-permute-done.6 = f32[512,512]{1,0:T(8,128)S(1)} collective-permute-done((f32[512,512]{1,0:T(8,128)S(1)}, f32[512,512]{1,0:T(8,128)S(1)}, u32[]{:S(2)}, u32[]{:S(2)}) %collective-permute-start.6) | collective-permute-done | bytes 1048608 | tf_op jit(solution)/shard_map/ppermute | solution.py:30
  198.6 1.2 dynamic-slice_add_fusion
  199.8 0.0 reduce-scatter.5.cloned.1.call-update
  199.8 0.0 reduce-scatter.3.cloned.1.call-done
  199.8 26.5 %reduce-scatter.5.cloned.1.call-done = f32[128,512]{1,0:T(8,128)} async-done(((f32[512,512]{1,0:T(8,128)}), f32[128,512]{1,0:T(8,128)}) %reduce-scatter.5.cloned.1.call-update) | async-done | bytes 262160 | tf_op jit(solution)/shard_map/reduce_scatter | solution.py:182
  (10 shorter events, 0.1 us)
Async XLA Ops:
  7.2 0.7 copy-start
  7.2 8.3 %copy-start.1 = (bf16[1,1,2,128,1024]{4,3,2,1,0:T(8,128)(2,1)S(1)}, bf16[1,1,2,128,1024]{4,3,2,1,0:T(8,128)(2,1)}, u32[]{:S(2)}) copy-start(bf16[1,1,2,128,1024]{4,3,2,1,0:T(8,128)(2,1)} %param.14) | copy-start | bytes 1572868
  7.2 9.1 %copy-start.4 = (bf16[1,2,128,1024]{3,2,1,0:T(8,128)(2,1)S(1)}, bf16[1,2,128,1024]{3,2,1,0:T(8,128)(2,1)}, u32[]{:S(2)}) copy-start(bf16[1,2,128,1024]{3,2,1,0:T(8,128)(2,1)} %param.17) | copy-start | bytes 1572868
  7.2 192.6 %reduce-scatter.3.cloned.1.call-start = ((), (), s32[]{:S(2)}) async-start(), calls=%async_computation.2 | async-start | bytes 1310720 | tf_op jit(solution)/shard_map/reduce_scatter | solution.py:181
  11.4 77.0 %collective-permute-start.1 = (bf16[2,128,1024]{2,1,0:T(8,128)(2,1)}, bf16[2,128,1024]{2,1,0:T(8,128)(2,1)}, u32[]{:S(2)}, u32[]{:S(2)}) collective-permute-start(bf16[2,128,1024]{2,1,0:T(8,128)(2,1)} %get-tuple-element.267), channel_id=1, source_target_pairs={{0,4},{2,6},{4,0},{6,2},{1,5},{3,7},{5,1},{7,3},{8,12},{10,14},{12... | collective-permute-start | bytes 1572872 | tf_op jit(solution)/shard_map/ppermute | solution.py:12
  17.1 33.0 %collective-permute-start = (bf16[128,1024]{1,0:T(8,128)(2,1)}, bf16[128,1024]{1,0:T(8,128)(2,1)S(1)}, u32[]{:S(2)}, u32[]{:S(2)}) collective-permute-start(bf16[128,1024]{1,0:T(8,128)(2,1)} %get-tuple-element.372), channel_id=1, source_target_pairs={{0,4},{2,6},{4,0},{6,2},{1,5},{3,7},{5,1},{7,3},{8,12},{10,14},{12... | collective-permute-start | bytes 786440 | tf_op jit(solution)/shard_map/while/body/eval_jaxpr/ppermute | solution.py:12
  50.1 21.1 %collective-permute-start = (bf16[128,1024]{1,0:T(8,128)(2,1)}, bf16[128,1024]{1,0:T(8,128)(2,1)S(1)}, u32[]{:S(2)}, u32[]{:S(2)}) collective-permute-start(bf16[128,1024]{1,0:T(8,128)(2,1)} %get-tuple-element.372), channel_id=1, source_target_pairs={{0,4},{2,6},{4,0},{6,2},{1,5},{3,7},{5,1},{7,3},{8,12},{10,14},{12... | collective-permute-start | bytes 786440 | tf_op jit(solution)/shard_map/while/body/eval_jaxpr/ppermute | solution.py:12
  85.1 20.6 %collective-permute-start.2 = (bf16[2,128,1024]{2,1,0:T(8,128)(2,1)S(1)}, bf16[2,128,1024]{2,1,0:T(8,128)(2,1)S(1)}, u32[]{:S(2)}, u32[]{:S(2)}) collective-permute-start(bf16[2,128,1024]{2,1,0:T(8,128)(2,1)S(1)} %get-tuple-element.276), channel_id=1, source_target_pairs={{0,4},{2,6},{4,0},{6,2},{1,5},{3,7},{5,1},{7,3},{8,12},{10,14},{12... | collective-permute-start | bytes 1572872 | tf_op jit(solution)/shard_map/ppermute | solution.py:12
  113.5 3.7 %copy-start.3 = (bf16[2,128,1024]{2,1,0:T(8,128)(2,1)S(1)}, bf16[2,128,1024]{2,1,0:T(8,128)(2,1)}, u32[]{:S(2)}) copy-start(bf16[2,128,1024]{2,1,0:T(8,128)(2,1)} %get-tuple-element.277) | copy-start | bytes 1572868
  115.0 43.2 %collective-permute-start.3 = (f32[512,512]{1,0:T(8,128)}, f32[512,512]{1,0:T(8,128)}, u32[]{:S(2)}, u32[]{:S(2)}) collective-permute-start(f32[512,512]{1,0:T(8,128)} %constant_dynamic-slice_fusion.1), channel_id=1, source_target_pairs={{0,2},{2,0},{4,6},{6,4},{1,3},{3,1},{5,7},{7,5},{8,10},{10,8},{12,... | collective-permute-start | bytes 3145736 | tf_op jit(solution)/shard_map/ppermute | solution.py:30
  115.0 35.1 %collective-permute-start.5 = (bf16[2,128,1024]{2,1,0:T(8,128)(2,1)}, bf16[2,128,1024]{2,1,0:T(8,128)(2,1)}, u32[]{:S(2)}, u32[]{:S(2)}) collective-permute-start(bf16[2,128,1024]{2,1,0:T(8,128)(2,1)} %get-tuple-element.275), channel_id=1, source_target_pairs={{0,4},{2,6},{4,0},{6,2},{1,5},{3,7},{5,1},{7,3},{8,12},{10,14},{12... | collective-permute-start | bytes 1572872 | tf_op jit(solution)/shard_map/ppermute | solution.py:12
  117.2 44.5 %collective-permute-start.4 = (bf16[2,128,1024]{2,1,0:T(8,128)(2,1)S(1)}, bf16[2,128,1024]{2,1,0:T(8,128)(2,1)}, u32[]{:S(2)}, u32[]{:S(2)}) collective-permute-start(bf16[2,128,1024]{2,1,0:T(8,128)(2,1)S(1)} %copy-done.3), channel_id=1, source_target_pairs={{0,4},{2,6},{4,0},{6,2},{1,5},{3,7},{5,1},{7,3},{8,12},{10,14},{12... | collective-permute-start | bytes 1572872 | tf_op jit(solution)/shard_map/ppermute | solution.py:12
  151.8 9.8 %copy-start.2 = (bf16[2,128,1024]{2,1,0:T(8,128)(2,1)S(1)}, bf16[2,128,1024]{2,1,0:T(8,128)(2,1)}, u32[]{:S(2)}) copy-start(bf16[2,128,1024]{2,1,0:T(8,128)(2,1)} %get-tuple-element.278) | copy-start | bytes 1572868
  160.7 65.7 %reduce-scatter.5.cloned.1.call-start = ((), (), s32[]{:S(2)}) async-start(), calls=%async_computation.3 | async-start | bytes 1310720 | tf_op jit(solution)/shard_map/reduce_scatter | solution.py:182
  179.8 18.8 %collective-permute-start.6 = (f32[512,512]{1,0:T(8,128)S(1)}, f32[512,512]{1,0:T(8,128)S(1)}, u32[]{:S(2)}, u32[]{:S(2)}) collective-permute-start(f32[512,512]{1,0:T(8,128)S(1)} %constant_dynamic-slice_fusion), channel_id=1, source_target_pairs={{0,2},{2,0},{4,6},{6,4},{1,3},{3,1},{5,7},{7,5},{8,10},{10,8},{12,... | collective-permute-start | bytes 3145736 | tf_op jit(solution)/shard_map/ppermute | solution.py:30
Sparse Core Ops, SparseCore 0:
  160.8 25.1 reduce-scatter.2
  199.9 26.3 reduce-scatter.4
where the time goes:
time: 234 us; the launch traced here: 233 us
  waiting for transfers between devices  137 us (59%)
  blocking collectives  31.5 us (13%)
  starting transfers between devices  16.8 us (7%)
  other arithmetic  16.3 us (7%)
  between operations  16.2 us (7%)
  matrix products  10.7 us (5%)
  local copies, waits for them, and re-layouts  3.85 us (2%)
    ppermute x6, waiting for transfers between devices, shifted(): return lax.ppermute(value, axis, pairs)  84.8 us
    reduce_scatter x1, waiting for transfers between devices, body(): lax.psum_scatter(mine_out + landed_out, 'pipe', scatter_dimension=0, tile...  26.5 us
    ppermute x2, waiting for transfers between devices, partner(): return lax.ppermute(block, axis, route)  25.2 us
    ppermute x6, starting transfers between devices, shifted(): return lax.ppermute(value, axis, pairs)  16.6 us
    all_gather x1, blocking collectives, body(): value_piece = lax.all_gather(value_own, 'tensor', axis=0, tiled=True)  8.92 us
    all_gather x1, blocking collectives, body(): unit_piece = lax.all_gather(unit_own, 'tensor', axis=0, tiled=True)  8.51 us
    all_gather x1, blocking collectives, body(): err_piece = lax.all_gather(err_own, 'tensor', axis=0, tiled=True)  7.04 us
    all_gather x1, blocking collectives, body(): grad_piece = lax.all_gather(grad_own, 'tensor', axis=0, tiled=True)  7.03 us
  transfers between devices with their start and end apart: 10, of which 8 were waited for; matrix products, arithmetic and copies ran while one was open for 10% of the time, Pallas kernels for 0%

commit v1 on v0

--- a/solution.py
+++ b/solution.py
@@ -162,8 +162,11 @@
     out_cols = model_width // tensors
     unit_piece = lax.all_gather(unit_own, "tensor", axis=0, tiled=True)
     value_piece = lax.all_gather(value_own, "tensor", axis=0, tiled=True)
-    err_piece = lax.all_gather(err_own, "tensor", axis=0, tiled=True)
-    grad_piece = lax.all_gather(grad_own, "tensor", axis=0, tiled=True)
+    err_piece, grad_piece = jnp.split(
+        lax.all_gather(jnp.concatenate([err_own, grad_own], axis=1), "tensor", axis=0, tiled=True),
+        [err_own.shape[1]],
+        axis=1,
+    )
     err_cols = lax.dynamic_slice_in_dim(err_piece, tensor_index * in_cols, in_cols, 1)
     grad_cols = lax.dynamic_slice_in_dim(grad_piece, tensor_index * out_cols, out_cols, 1)
     totals = (

time: 234 us -> 248 us (1.060)
  waiting for transfers between devices: 137 us -> 161 us
  blocking collectives: 31.5 us -> 15.2 us
  starting transfers between devices: 16.8 us -> 21.4 us
    ppermute x2, waiting for transfers between devices: 25.2 us -> 55.8 us  [partner(): return lax.ppermute(block, axis, route)]
    reduce_scatter x1, waiting for transfers between devices: 26.5 us -> 0.02 us  [body(): lax.psum_scatter(mine_out + landed_out, 'pipe', scatter_dimension=0, tile...]
    reduce_scatter x1, waiting for transfers between devices: 0.02 us -> 24.9 us  [body(): lax.psum_scatter(mine_in + landed_in, 'pipe', scatter_dimension=0, tiled=...]
    all_gather x2 -> x0, blocking collectives: 14.1 us -> none  [the longest x1 7.04 us: body(): err_piece = lax.all_gather(err_own, 'tensor', axis=0, tiled=True)]
    ppermute x6, waiting for transfers between devices: 84.8 us -> 80 us  [shifted(): return lax.ppermute(value, axis, pairs)]
    add x4 -> x2, other arithmetic: 5.58 us -> 1.41 us  [route_items(): jnp.where(keep_mask[:, None, None], member, jnp.zeros_like(member)) + landed]
    squeeze x0 -> x2, other arithmetic: none -> 3.25 us  [the longest x1 1.63 us: body(): err_own = lax.dynamic_index_in_dim(err_got, owner_slot, 0, keepdims=False)]
  transfers between devices with their start and end apart: 10 -> 11, of which waited for: 8 -> 8; matrix products, arithmetic and copies ran while one was open for 10% -> 3% of each run, Pallas kernels for 0% -> 0%
where the time goes in v1:
time: 248 us; the launch traced here: 247 us
  waiting for transfers between devices  161 us (65%)
  starting transfers between devices  21.4 us (9%)
  other arithmetic  16.3 us (7%)
  between operations  15.9 us (6%)
  blocking collectives  15.2 us (6%)
  matrix products  10.3 us (4%)
  local copies, waits for them, and re-layouts  5.85 us (2%)
    ppermute x6, waiting for transfers between devices, shifted(): return lax.ppermute(value, axis, pairs)  80 us
    ppermute x2, waiting for transfers between devices, partner(): return lax.ppermute(block, axis, route)  55.8 us
    reduce_scatter x1, waiting for transfers between devices, body(): lax.psum_scatter(mine_in + landed_in, 'pipe', scatter_dimension=0, tiled=...  24.9 us
    ppermute x6, starting transfers between devices, shifted(): return lax.ppermute(value, axis, pairs)  19.1 us
    all_gather x1, blocking collectives, body(): unit_piece = lax.all_gather(unit_own, 'tensor', axis=0, tiled=True)  8.14 us
    all_gather x1, blocking collectives, body(): value_piece = lax.all_gather(value_own, 'tensor', axis=0, tiled=True)  7.04 us
  transfers between devices with their start and end apart: 11, of which 8 were waited for; matrix products, arithmetic and copies ran while one was open for 3% of the time, Pallas kernels for 0%

profile of v1, /device:TPU:0, one launch (start us, length us, event | category | flops | bytes accessed | tf_op | source)
XLA Modules:
  0.0 247.0 jit_solution(18421038611431275906)
XLA Ops:
  7.2 0.0 copy-start
  7.2 0.0 copy-start.1
  7.2 0.0 copy-start.3
  7.2 0.0 all-gather.4.cloned.1.call-start
  7.3 0.6 copy-done
  7.9 0.1 bitcast_subtract_fusion
  7.9 1.2 fusion.28
  9.2 1.2 convert_divide_fusion
  10.4 0.6 dynamic_slice.45
  11.0 0.1 and_reduce_fusion.1
  11.1 1.1 broadcast_select_fusion.3
  12.2 0.0 copy-done.3
  12.2 0.7 select_bitcast_fusion
  12.9 0.1 broadcast.103
  13.0 0.1 broadcast.103.clone
  13.0 47.3 %while.17 = (s32[]{:T(128)}, bf16[128,1024]{1,0:T(8,128)(2,1)}, bf16[2,128,1024]{2,1,0:T(8,128)(2,1)S(1)}, bf16[2,128,1024]{2,1,0:T(8,128)(2,1)S(1)}, s32[]{:T(1...) while((s32[]{:T(128)}, bf16[128,1024]{1,0:T(8,128)(2,1)}, ...), condition=%wide.region_13.14_spmd, body=%wide.region_4.13_spmd.sunk | while | flops 1076625408 | bytes 18357668 | solution.py:137
  13.0 4.1 %collective-permute-start = (bf16[128,1024]{1,0:T(8,128)(2,1)}, bf16[128,1024]{1,0:T(8,128)(2,1)S(1)}, u32[]{:S(2)}, u32[]{:S(2)}) collective-permute-start(bf16[128,1024]{1,0:T(8,128)(2,1)} %get-tuple-element.374), channel_id=1, source_target_pairs={{0,4},{2,6},{4,0},{6,2},{1,5},{3,7},{5,1},{7,3},{8,12},{10,14},{12... | collective-permute-start | bytes 786440 | tf_op jit(solution)/shard_map/while/body/eval_jaxpr/ppermute | solution.py:12
  17.2 12.1 %collective-permute-done = bf16[128,1024]{1,0:T(8,128)(2,1)S(1)} collective-permute-done((bf16[128,1024]{1,0:T(8,128)(2,1)}, bf16[128,1024]{1,0:T(8,128)(2,1)S(1)}, u32[]{:S(2)}, u32[]{:S(2)}) %collective-permute-start) | collective-permute-done | bytes 262176 | tf_op jit(solution)/shard_map/while/body/eval_jaxpr/ppermute | solution.py:12
  29.3 9.6 %collective-permute-start = (bf16[128,1024]{1,0:T(8,128)(2,1)}, bf16[128,1024]{1,0:T(8,128)(2,1)S(1)}, u32[]{:S(2)}, u32[]{:S(2)}) collective-permute-start(bf16[128,1024]{1,0:T(8,128)(2,1)} %get-tuple-element.374), channel_id=1, source_target_pairs={{0,4},{2,6},{4,0},{6,2},{1,5},{3,7},{5,1},{7,3},{8,12},{10,14},{12... | collective-permute-start | bytes 786440 | tf_op jit(solution)/shard_map/while/body/eval_jaxpr/ppermute | solution.py:12
  38.9 11.6 %collective-permute-done = bf16[128,1024]{1,0:T(8,128)(2,1)S(1)} collective-permute-done((bf16[128,1024]{1,0:T(8,128)(2,1)}, bf16[128,1024]{1,0:T(8,128)(2,1)S(1)}, u32[]{:S(2)}, u32[]{:S(2)}) %collective-permute-start) | collective-permute-done | bytes 262176 | tf_op jit(solution)/shard_map/while/body/eval_jaxpr/ppermute | solution.py:12
  50.4 9.8 %conditional.4 = ((bf16[128,1024]{1,0:T(8,128)(2,1)}, bf16[2,128,1024]{2,1,0:T(8,128)(2,1)S(1)}, bf16[2,128,1024]{2,1,0:T(8,128)(2,1)S(1)})) conditional(s32[]{:T(128)} %convert_element_type.62, (bf16[128,1024]{1,0:T(8,128)(2,1)}, bf16[2,128,1024]{2,1,0:T(8,128)(2,1)S(1)}, bf16[2,128,1024]{2,1,0:T(8,128)(2,1)S(1)}) %tuple.70, (s32[]{:T(128)}, ...), branch_computations={%region_5.5_spmd, %region_6.0_spmd} | conditional | flops 1076625408 | bytes 17308844 | solution.py:123
  51.1 0.8 conditional
  51.1 0.7 stack.18
  52.5 6.7 %conditional.1 = (bf16[128,1024]{1,0:T(8,128)(2,1)}, bf16[1,128,1024]{2,1,0:T(8,128)(2,1)}) conditional(s32[]{:T(128)} %convert_element_type.36, bf16[128,1024]{1,0:T(8,128)(2,1)S(1)} %get-tuple-element.221, (bf16[128,1024]{1,0:T(8,128)(2,1)S(1)}, bf16[2,1024,1024]{2,1,0:T(8,128)(2,1)}, bf16[2,1024,1024]{2,1,0:T(8,128)(2,1)}, ...), branch_computations={%region_10.9_spmd, %region_11.11_spmd} | conditional | flops 538050560 | bytes 7605776 | solution.py:118
  52.5 3.1 %fusion.20 = bf16[128,1024]{1,0:T(8,128)(2,1)} fusion(bf16[128,1024]{1,0:T(8,128)(2,1)S(1)} %get-tuple-element.210, bf16[2,1024,1024]{2,1,0:T(8,128)(2,1)} %get-tuple-element.211), kind=kOutput, calls=%fused_computation.22 | convolution fusion | flops 268566528 | bytes 2621440 | tf_op jit(solution)/shard_map/while/body/eval_jaxpr/cond/branch_1_fun/cond/branch_1_fun/dot_general | solution.py:40
  55.6 2.6 %fusion.23 = (f32[128]{0:T(128)S(1)}, f32[128,1024]{1,0:T(8,128)S(1)}) fusion(f32[2,128,1024]{2,1,0:T(8,128)S(1)} %get-tuple-element.213, bf16[128,1024]{1,0:T(8,128)(2,1)} %fusion.20, bf16[2,1024,1024]{2,1,0:T(8,128)(2,1)} %get-tuple-element.212), kind=kOutput, calls=%fused_computation.25 | convolution fusion | flops 268697472 | bytes 3408384 | tf_op jit(solution)/shard_map/while/body/eval_jaxpr/cond/branch_1_fun/cond/branch_1_fun/dot_general | solution.py:43
  58.2 0.9 fusion.27
  59.1 1.1 pad_maximum_fusion
  60.3 3.7 %broadcast_select_fusion = (bf16[2,128,1024]{2,1,0:T(8,128)(2,1)S(1)}, bf16[2,128,1024]{2,1,0:T(8,128)(2,1)}, bf16[2,128,1024]{2,1,0:T(8,128)(2,1)S(1)}, bf16[2,128,1024]{2,1,0:T(8,128)(2,1)S(1)}) fusion(pred[2]{0:T(512)(128)(4,1)S(1)} %get-tuple-element.246, bf16[2,128,1024]{2,1,0:T(8,128)(2,1)S(1)} %get-tuple-element.243, ...), kind=kOutput, calls=%fused_computation.45 | convolution fusion | flops 537919488 | bytes 7864322 | tf_op jit(solution)/shard_map/kre,kea->kra/dot_general | solution.py:95
  64.0 0.0 collective-permute-start.2
  64.0 2.9 %collective-permute-start.3 = (bf16[2,128,1024]{2,1,0:T(8,128)(2,1)S(1)}, bf16[2,128,1024]{2,1,0:T(8,128)(2,1)}, u32[]{:S(2)}, u32[]{:S(2)}) collective-permute-start(bf16[2,128,1024]{2,1,0:T(8,128)(2,1)S(1)} %get-tuple-element.279), channel_id=1, source_target_pairs={{0,4},{2,6},{4,0},{6,2},{1,5},{3,7},{5,1},{7,3},{8,12},{10,14},{12... | collective-permute-start | bytes 1572872 | tf_op jit(solution)/shard_map/ppermute | solution.py:12
  66.9 0.7 fusion.42
  69.5 0.6 dynamic-slice.1
  70.1 30.0 %collective-permute-done.2 = bf16[2,128,1024]{2,1,0:T(8,128)(2,1)} collective-permute-done((bf16[2,128,1024]{2,1,0:T(8,128)(2,1)}, bf16[2,128,1024]{2,1,0:T(8,128)(2,1)}, u32[]{:S(2)}, u32[]{:S(2)}) %collective-permute-start.2) | collective-permute-done | bytes 524320 | tf_op jit(solution)/shard_map/ppermute | solution.py:12
  100.2 1.6 fusion.34
  101.8 5.0 %collective-permute-done.3 = bf16[2,128,1024]{2,1,0:T(8,128)(2,1)} collective-permute-done((bf16[2,128,1024]{2,1,0:T(8,128)(2,1)S(1)}, bf16[2,128,1024]{2,1,0:T(8,128)(2,1)}, u32[]{:S(2)}, u32[]{:S(2)}) %collective-permute-start.3) | collective-permute-done | bytes 524320 | tf_op jit(solution)/shard_map/ppermute | solution.py:12
  106.8 1.6 fusion.33
  108.4 0.9 pad_maximum_fusion.2
  109.3 0.0 all-gather.4.cloned.1.call-update
  109.3 0.0 reduce-scatter.5.cloned.1.call-start
  109.3 0.1 collective-permute-start.5
  109.4 21.3 %collective-permute-done.5 = bf16[2,128,1024]{2,1,0:T(8,128)(2,1)S(1)} collective-permute-done((bf16[2,128,1024]{2,1,0:T(8,128)(2,1)S(1)}, bf16[2,128,1024]{2,1,0:T(8,128)(2,1)S(1)}, u32[]{:S(2)}, u32[]{:S(2)}) %collective-permute-start.5) | collective-permute-done | bytes 524320 | tf_op jit(solution)/shard_map/ppermute | solution.py:12
  130.7 0.7 dynamic-slice_add_fusion.2
  131.4 7.0 %all-gather.1 = bf16[1,256,1024]{2,1,0:T(8,128)(2,1)S(1)} all-gather(bf16[1,128,1024]{2,1,0:T(8,128)(2,1)S(1)} %dynamic-slice_add_fusion.2), channel_id=3, replica_groups=mesh['pipe'=4,'section'=4,'tensor'=2] {'tensor'}, dimensions={1}, use_global_device_ids=true | all-gather | bytes 786432 | tf_op jit(solution)/shard_map/all_gather | solution.py:164
  138.4 2.1 fusion.47
  140.5 0.5 fusion.29
  141.0 1.0 constant_dynamic-slice_fusion
  142.0 2.1 collective-permute-start.6
  144.1 2.4 collective-permute-start.1
  146.5 32.3 %collective-permute-done.6 = f32[512,512]{1,0:T(8,128)} collective-permute-done((f32[512,512]{1,0:T(8,128)}, f32[512,512]{1,0:T(8,128)}, u32[]{:S(2)}, u32[]{:S(2)}) %collective-permute-start.6) | collective-permute-done | bytes 1048608 | tf_op jit(solution)/shard_map/ppermute | solution.py:30
  178.8 2.4 dynamic-slice_add_fusion
  181.3 0.0 reduce-scatter.5.cloned.1.call-update
  181.3 0.0 reduce-scatter.3.cloned.1.call-start
  181.4 0.0 collective-permute-done.1
  181.4 0.7 dynamic-slice_add_fusion.5
  182.1 8.1 %all-gather = bf16[1,256,1024]{2,1,0:T(8,128)(2,1)S(1)} all-gather(bf16[1,128,1024]{2,1,0:T(8,128)(2,1)S(1)} %dynamic-slice_add_fusion.5), channel_id=2, replica_groups=mesh['pipe'=4,'section'=4,'tensor'=2] {'tensor'}, dimensions={1}, use_global_device_ids=true | all-gather | bytes 786432 | tf_op jit(solution)/shard_map/all_gather | solution.py:163
  190.3 0.5 fusion.31
  190.7 0.1 constant_dynamic-slice_fusion.1
  190.8 0.1 collective-permute-start.4
  190.9 23.5 %collective-permute-done.4 = f32[512,512]{1,0:T(8,128)S(1)} collective-permute-done((f32[512,512]{1,0:T(8,128)S(1)}, f32[512,512]{1,0:T(8,128)S(1)}, u32[]{:S(2)}, u32[]{:S(2)}) %collective-permute-start.4) | collective-permute-done | bytes 1048608 | tf_op jit(solution)/shard_map/ppermute | solution.py:30
  214.3 1.2 dynamic-slice_add_fusion.1
  215.5 0.0 reduce-scatter.3.cloned.1.call-update
  215.6 0.0 reduce-scatter.5.cloned.1.call-done
  215.6 24.9 %reduce-scatter.3.cloned.1.call-done = f32[128,512]{1,0:T(8,128)} async-done(((f32[512,512]{1,0:T(8,128)}), f32[128,512]{1,0:T(8,128)}) %reduce-scatter.3.cloned.1.call-update) | async-done | bytes 262160 | tf_op jit(solution)/shard_map/reduce_scatter | solution.py:184
  (11 shorter events, 0.1 us)
Async XLA Ops:
  7.2 0.7 copy-start
  7.2 3.9 %copy-start.1 = (bf16[1,1,2,128,1024]{4,3,2,1,0:T(8,128)(2,1)S(1)}, bf16[1,1,2,128,1024]{4,3,2,1,0:T(8,128)(2,1)}, u32[]{:S(2)}) copy-start(bf16[1,1,2,128,1024]{4,3,2,1,0:T(8,128)(2,1)} %param.14) | copy-start | bytes 1572868
  7.2 5.0 %copy-start.3 = (bf16[1,2,128,1024]{3,2,1,0:T(8,128)(2,1)S(1)}, bf16[1,2,128,1024]{3,2,1,0:T(8,128)(2,1)}, u32[]{:S(2)}) copy-start(bf16[1,2,128,1024]{3,2,1,0:T(8,128)(2,1)} %param.17) | copy-start | bytes 1572868
  7.2 131.2 %all-gather.4.cloned.1.call-start = ((), (), s32[]{:S(2)}) async-start(), calls=%async_computation.2 | async-start | bytes 1572864 | tf_op jit(solution)/shard_map/all_gather | solution.py:166
  13.0 16.3 %collective-permute-start = (bf16[128,1024]{1,0:T(8,128)(2,1)}, bf16[128,1024]{1,0:T(8,128)(2,1)S(1)}, u32[]{:S(2)}, u32[]{:S(2)}) collective-permute-start(bf16[128,1024]{1,0:T(8,128)(2,1)} %get-tuple-element.374), channel_id=1, source_target_pairs={{0,4},{2,6},{4,0},{6,2},{1,5},{3,7},{5,1},{7,3},{8,12},{10,14},{12... | collective-permute-start | bytes 786440 | tf_op jit(solution)/shard_map/while/body/eval_jaxpr/ppermute | solution.py:12
  29.3 21.1 %collective-permute-start = (bf16[128,1024]{1,0:T(8,128)(2,1)}, bf16[128,1024]{1,0:T(8,128)(2,1)S(1)}, u32[]{:S(2)}, u32[]{:S(2)}) collective-permute-start(bf16[128,1024]{1,0:T(8,128)(2,1)} %get-tuple-element.374), channel_id=1, source_target_pairs={{0,4},{2,6},{4,0},{6,2},{1,5},{3,7},{5,1},{7,3},{8,12},{10,14},{12... | collective-permute-start | bytes 786440 | tf_op jit(solution)/shard_map/while/body/eval_jaxpr/ppermute | solution.py:12
  64.0 36.2 %collective-permute-start.2 = (bf16[2,128,1024]{2,1,0:T(8,128)(2,1)}, bf16[2,128,1024]{2,1,0:T(8,128)(2,1)}, u32[]{:S(2)}, u32[]{:S(2)}) collective-permute-start(bf16[2,128,1024]{2,1,0:T(8,128)(2,1)} %get-tuple-element.278), channel_id=1, source_target_pairs={{0,4},{2,6},{4,0},{6,2},{1,5},{3,7},{5,1},{7,3},{8,12},{10,14},{12... | collective-permute-start | bytes 1572872 | tf_op jit(solution)/shard_map/ppermute | solution.py:12
  64.0 42.8 %collective-permute-start.3 = (bf16[2,128,1024]{2,1,0:T(8,128)(2,1)S(1)}, bf16[2,128,1024]{2,1,0:T(8,128)(2,1)}, u32[]{:S(2)}, u32[]{:S(2)}) collective-permute-start(bf16[2,128,1024]{2,1,0:T(8,128)(2,1)S(1)} %get-tuple-element.279), channel_id=1, source_target_pairs={{0,4},{2,6},{4,0},{6,2},{1,5},{3,7},{5,1},{7,3},{8,12},{10,14},{12... | collective-permute-start | bytes 1572872 | tf_op jit(solution)/shard_map/ppermute | solution.py:12
  109.3 106.3 %reduce-scatter.5.cloned.1.call-start = ((), (), s32[]{:S(2)}) async-start(), calls=%async_computation.4 | async-start | bytes 1310720 | tf_op jit(solution)/shard_map/reduce_scatter | solution.py:185
  109.3 21.4 %collective-permute-start.5 = (bf16[2,128,1024]{2,1,0:T(8,128)(2,1)S(1)}, bf16[2,128,1024]{2,1,0:T(8,128)(2,1)S(1)}, u32[]{:S(2)}, u32[]{:S(2)}) collective-permute-start(bf16[2,128,1024]{2,1,0:T(8,128)(2,1)S(1)} %get-tuple-element.277), channel_id=1, source_target_pairs={{0,4},{2,6},{4,0},{6,2},{1,5},{3,7},{5,1},{7,3},{8,12},{10,14},{12... | collective-permute-start | bytes 1572872 | tf_op jit(solution)/shard_map/ppermute | solution.py:12
  142.0 36.8 %collective-permute-start.6 = (f32[512,512]{1,0:T(8,128)}, f32[512,512]{1,0:T(8,128)}, u32[]{:S(2)}, u32[]{:S(2)}) collective-permute-start(f32[512,512]{1,0:T(8,128)} %constant_dynamic-slice_fusion), channel_id=1, source_target_pairs={{0,2},{2,0},{4,6},{6,4},{1,3},{3,1},{5,7},{7,5},{8,10},{10,8},{12,... | collective-permute-start | bytes 3145736 | tf_op jit(solution)/shard_map/ppermute | solution.py:30
  144.1 37.2 %collective-permute-start.1 = (bf16[2,128,1024]{2,1,0:T(8,128)(2,1)}, bf16[2,128,1024]{2,1,0:T(8,128)(2,1)S(1)}, u32[]{:S(2)}, u32[]{:S(2)}) collective-permute-start(bf16[2,128,1024]{2,1,0:T(8,128)(2,1)} %get-tuple-element.267), channel_id=1, source_target_pairs={{0,4},{2,6},{4,0},{6,2},{1,5},{3,7},{5,1},{7,3},{8,12},{10,14},{12... | collective-permute-start | bytes 1572872 | tf_op jit(solution)/shard_map/ppermute | solution.py:12
  181.3 9.0 %copy-start.2 = (bf16[256,1024]{1,0:T(8,128)(2,1)S(1)}, bf16[256,1024]{1,0:T(8,128)(2,1)}, u32[]{:S(2)}) copy-start(bf16[256,1024]{1,0:T(8,128)(2,1)} %get-tuple-element.276) | copy-start | bytes 1572868
  181.3 59.2 %reduce-scatter.3.cloned.1.call-start = ((), (), s32[]{:S(2)}) async-start(), calls=%async_computation.3 | async-start | bytes 1310720 | tf_op jit(solution)/shard_map/reduce_scatter | solution.py:184
  190.8 23.5 %collective-permute-start.4 = (f32[512,512]{1,0:T(8,128)S(1)}, f32[512,512]{1,0:T(8,128)S(1)}, u32[]{:S(2)}, u32[]{:S(2)}) collective-permute-start(f32[512,512]{1,0:T(8,128)S(1)} %constant_dynamic-slice_fusion.1), channel_id=1, source_target_pairs={{0,2},{2,0},{4,6},{6,4},{1,3},{3,1},{5,7},{7,5},{8,10},{10,8},{12,... | collective-permute-start | bytes 3145736 | tf_op jit(solution)/shard_map/ppermute | solution.py:30
Sparse Core Ops, SparseCore 0:
  109.4 24.2 all-gather.3
  181.4 25.0 reduce-scatter.4
  215.7 24.7 reduce-scatter.2
